TPU v7x, 32 devices: a whole 2x2x4 slice. The times are simulated.
32 devices in a mesh: ka: 2 (over core), pair: 16 (over z, y, x).
Axes of the slice: x: 2, y: 2, z: 4, core: 2. Of those that a mesh axis runs over, the one named last changes fastest.
Arguments:
- cond_orbitals: bfloat16 [2, 2048, 2048], P('ka', 'pair'), may hold values from -6 to 6
- cond_energy: float32 [2, 2048], P('ka', 'pair'), may hold values from 0.5 to 8
- val_orbitals: bfloat16 [32, 2048], P(('ka', 'pair')), may hold values from -6 to 6
- val_energy: bfloat16 [32], P(('ka', 'pair')), may hold values from -8 to -0.5
- val_slots: int32 [2, 16, 16], P('ka', 'pair'), may hold values from 0 to 31
- owner_count: int32 [2, 16], P('ka', 'pair'), may hold values from 1 to 16, as said below
Outputs:
- response: float32 [2, 2048, 512], P('ka', 'pair')
Inputs may be any that keep to these rules, and one draw needn't show every extreme that they name: `owner_count`: in every lane some owner has exactly 16 live slots.
All inputs are finite; a program needn't handle non-finite values.
Results may differ from a plain program's by a relative error of at most 0.0047.
The roundings to bfloat16 on the way count: a program that leaves them out, or rounds other values in their place, can miss the bound.
Values may be sent and summed in bfloat16 or wider, within the bound.
A program may use at most 64 MiB of HBM per device.

v0:
```python
import jax
import jax.numpy as jnp
from jax import lax
from jax.sharding import PartitionSpec as P

BC = 128
GA = 16
GB = 128
WIN = 512
SLOTS = 16


def cosine_table(length):
    freq = lax.iota(jnp.float32, length)[:, None]
    point = lax.iota(jnp.float32, length)[None, :]
    factor = jnp.where(freq == 0, jnp.sqrt(1.0 / length), jnp.sqrt(2.0 / length))
    return (factor * jnp.cos(jnp.pi * (point + 0.5) * freq / length)).astype(jnp.bfloat16)


def owner_terms(picked, e_pick, live, cond_block, e_cond, table_a, table_b):
    slots = picked.shape[0]
    pair_real = (
        picked[:, None, :].astype(jnp.float32) * cond_block[None].astype(jnp.float32)
    ).astype(jnp.bfloat16)
    count = slots * cond_block.shape[0]
    rows = pair_real.reshape(count * GA, GB)
    first = jnp.dot(rows, table_b.T, preferred_element_type=jnp.float32).astype(jnp.bfloat16)
    first = first.reshape(count, GA, GB)
    moved = jnp.einsum("ja,pak->pjk", table_a, first, preferred_element_type=jnp.float32)
    moved = moved.astype(jnp.bfloat16).reshape(count, GA * GB)
    weight = live[:, None] * 2.0 / (e_cond[None, :] - e_pick[:, None])
    weighted = (moved[:, :WIN].astype(jnp.float32) * weight.reshape(count, 1)).astype(jnp.bfloat16)
    return (moved, weighted)


def shards(cond_orbitals, cond_energy, val_orbitals, val_energy, val_slots, owner_count):
    cond_block = lax.all_to_all(cond_orbitals, "pair", split_axis=2, concat_axis=1, tiled=True)[0].T
    all_orb, all_energy = (
        lax.all_gather(val_orbitals, ("ka", "pair"), axis=0, tiled=True),
        lax.all_gather(val_energy, ("ka", "pair"), axis=0, tiled=True),
    )
    slots = val_slots[0, 0]
    picked = jnp.take(all_orb, slots, axis=0)
    e_pick = jnp.take(all_energy, slots).astype(jnp.float32)
    live = (lax.iota(jnp.int32, slots.shape[0]) < owner_count[0, 0]).astype(jnp.float32)
    moved, weighted = owner_terms(
        picked, e_pick, live, cond_block, cond_energy[0], cosine_table(GA), cosine_table(GB)
    )
    owners = lax.axis_size("pair")
    mine = lax.psum_scatter(
        lax.dot_general(
            moved, weighted, (((0,), (0,)), ((), ())), preferred_element_type=jnp.float32
        ),
        "pair",
        scatter_dimension=0,
        tiled=True,
    )
    scale = 2.0 / (SLOTS * BC * owners)
    return (mine * scale)[None]


def solution(mesh):
    return jax.shard_map(
        shards,
        mesh=mesh,
        in_specs=(
            P("ka", "pair", None),
            P("ka", "pair"),
            P(("ka", "pair"), None),
            P(("ka", "pair")),
            P("ka", "pair", None),
            P("ka", "pair"),
        ),
        out_specs=P("ka", "pair", None),
        check_vma=False,
    )
```

profile of v0, /device:TPU:0, one launch (start us, length us, event | category | flops | bytes accessed | tf_op | source)
XLA Modules:
  0.0 298.1 jit_solution(10170052519686423794)
XLA Ops:
  6.5 2.3 copy.15
  8.9 0.5 broadcast.173
  9.4 11.5 %reduce = bf16[2048,128]{1,0:T(8,128)(2,1)S(1)} reduce(bf16[2048,1,128]{2,1,0:T(2,128)(2,1)S(1)} %bitcast.43, bf16[]{:T(256)} %broadcast.173), dimensions={1}, to_apply=%bitcast.30.reduce_sub_computation | reduce | bytes 1048578
  20.9 0.9 reshape.162
  21.8 8.3 %all-to-all-start = ((bf16[16,2,8192]{2,1,0:T(2,128)(2,1)}), bf16[16,2,8192]{2,1,0:T(2,128)(2,1)S(1)}, u32[]{:S(2)}, u32[]{:S(2)}) async-start(bf16[16,2,8192]{2,1,0:T(2,128)(2,1)} %reshape.162), calls=%async_computation | async-start | bytes 1048576 | tf_op jit(solution)/shard_map/all_to_all | solution.py:37
  30.2 0.0 reduce-scatter.2.cloned.1.call-start
  30.3 0.7 fusion.11
  31.6 0.1 dynamic-update-slice
  31.7 41.0 %all-reduce = bf16[32]{0:T(256)(128)(2,1)S(1)} all-reduce(bf16[32]{0:T(256)(128)(2,1)S(1)} %dynamic-update-slice), channel_id=1, replica_groups=mesh['ka'=2,'pair'=16] {'ka','pair'}, use_global_device_ids=true, to_apply=%add | all-reduce | flops 32 | bytes 128
  72.7 67.5 %all-gather = bf16[32,1,2048]{2,1,0:T(2,128)(2,1)S(1)} all-gather(bf16[1,1,2048]{2,1,0:T(2,128)(2,1)} %bitcast.47), channel_id=1, replica_groups=mesh['ka'=2,'pair'=16] {'ka','pair'}, dimensions={0}, use_global_device_ids=true | all-gather | bytes 135168 | tf_op jit(solution)/shard_map/all_gather | solution.py:39
  140.2 0.1 copy.24
  140.3 0.7 gather_fusion.1
  141.0 0.6 gather_fusion
  142.2 0.7 select_convert_fusion.1
  142.9 0.7 divide_bitcast_fusion
  143.6 0.1 select_convert_fusion
  143.7 0.0 all-to-all-done
  143.7 0.5 reshape.163
  144.3 0.1 copy.16
  144.3 0.1 convert_bitcast_fusion
  144.4 0.3 copy.17
  144.8 0.3 copy.18
  145.1 5.4 %multiply_convert_fusion = bf16[16,128,2048]{2,1,0:T(8,128)(2,1)} fusion(f32[128,2048]{1,0:T(8,128)S(1)} %copy.18, f32[16,2048]{1,0:T(8,128)S(1)} %select_convert_fusion), kind=kLoop, calls=%fused_computation.3 | loop fusion | flops 8388608 | bytes 9568256 | tf_op jit(solution)/shard_map/convert_element_type | solution.py:24
  150.5 13.5 %convert_element_type.68 = bf16[32768,128]{1,0:T(8,128)(2,1)} reshape(bf16[16,128,2048]{2,1,0:T(8,128)(2,1)} %multiply_convert_fusion) | data formatting | bytes 16777216 | tf_op jit(solution)/shard_map/convert_element_type | solution.py:24
  164.0 5.9 %convolution_convert_fusion = bf16[32768,128]{1,0:T(8,128)(2,1)S(1)} fusion(bf16[32768,128]{1,0:T(8,128)(2,1)} %convert_element_type.68, f32[128]{0:T(128)S(1)} %get-tuple-element.8, f32[128]{0:T(128)S(1)} %get-tuple-element.7), kind=kOutput, calls=%fused_computation.2 | convolution fusion | flops 1078001664 | bytes 16778240 | tf_op jit(solution)/shard_map/dot_general | solution.py:27
  169.9 5.6 %convolution_convert_fusion.1 = bf16[2048,128,16]{1,2,0:T(8,128)(2,1)} fusion(bf16[2048,16,128]{2,1,0:T(8,128)(2,1)S(1)} %bitcast.39, f32[16]{0:T(128)S(1)} %get-tuple-element.10, f32[16]{0:T(128)S(1)} %get-tuple-element.9), kind=kOutput, calls=%fused_computation.5 | convolution fusion | flops 138413056 | bytes 16777344 | tf_op jit(solution)/shard_map/ja,pak->pjk/dot_general | solution.py:29
  175.5 10.9 %copy.23 = bf16[256,8,16,128]{3,1,2,0:T(8,128)(2,1)} copy(bf16[256,8,16,128]{3,2,1,0:T(8,128)(2,1)} %bitcast.40) | data formatting | bytes 16777216
  186.4 10.6 %fusion = f32[2048,512]{1,0:T(8,128)} fusion(bf16[2048,2048]{1,0:T(8,128)(2,1)} %bitcast.41, f32[2048]{0:T(1024)S(1)} %divide_bitcast_fusion), kind=kOutput, calls=%fused_computation.7 | convolution fusion | flops 4298113024 | bytes 14688256 | tf_op jit(solution)/shard_map/dot_general | solution.py:51
  197.0 0.0 reduce-scatter.2.cloned.1.call-update
  197.0 92.6 %reduce-scatter.2.cloned.1.call-done = f32[128,512]{1,0:T(8,128)} async-done(((f32[2048,512]{1,0:T(8,128)}), f32[128,512]{1,0:T(8,128)}) %reduce-scatter.2.cloned.1.call-update) | async-done | bytes 262160 | tf_op jit(solution)/shard_map/reduce_scatter | solution.py:50
  289.6 1.7 multiply_bitcast_fusion
  (5 shorter events, 0.0 us)
Async XLA Ops:
  21.8 121.9 %all-to-all-start = ((bf16[16,2,8192]{2,1,0:T(2,128)(2,1)}), bf16[16,2,8192]{2,1,0:T(2,128)(2,1)S(1)}, u32[]{:S(2)}, u32[]{:S(2)}) async-start(bf16[16,2,8192]{2,1,0:T(2,128)(2,1)} %reshape.162), calls=%async_computation | async-start | bytes 1048576 | tf_op jit(solution)/shard_map/all_to_all | solution.py:37
  30.2 259.4 %reduce-scatter.2.cloned.1.call-start = ((), (), s32[]{:S(2)}) async-start(), calls=%async_computation.2 | async-start | bytes 4456448 | tf_op jit(solution)/shard_map/reduce_scatter | solution.py:50
Sparse Core Ops, SparseCore 0:
  197.1 92.4 reduce-scatter.1
where the time goes:
time: 299 us; the launch traced here: 298 us
  blocking collectives  108 us (36%)
  waiting for transfers between devices  92.6 us (31%)
  local copies, waits for them, and re-layouts  30.9 us (10%)
  matrix products  22.1 us (7%)
  other arithmetic  20.8 us (7%)
  between operations  14.8 us (5%)
  starting transfers between devices  8.38 us (3%)
    reduce_scatter x1, waiting for transfers between devices, shards(): lax.psum_scatter(lax.dot_general(moved, weighted, (((0,), (0,)), ((), ())...  92.6 us
    all_gather x1, blocking collectives, shards(): lax.all_gather(val_orbitals, ('ka', 'pair'), axis=0, tiled=True)  67.5 us
    unnamed x1, blocking collectives  41 us
    unnamed x8, local copies, waits for them, and re-layouts  15.4 us
    convert_element_type x1, local copies, waits for them, and re-layouts, owner_terms(): pair_real = (picked[:, None, :].astype(jnp.float32) * cond_block[None].as...  13.5 us
    unnamed x1, other arithmetic  11.5 us
    dot_general x1, matrix products, shards(): lax.dot_general(moved, weighted, (((0,), (0,)), ((), ())), preferred_elem...  10.6 us
    all_to_all x1, starting transfers between devices, shards(): lax.all_to_all(cond_orbitals, 'pair', split_axis=2, concat_axis=1, tiled=...  8.34 us
  transfers between devices with their start and end apart: 2, of which 1 were waited for; matrix products, arithmetic and copies ran while one was open for 1% of the time, Pallas kernels for 0%

commit v1 on v0

--- a/solution.py
+++ b/solution.py
@@ -8,6 +8,28 @@
 GB = 128
 WIN = 512
 SLOTS = 16
+
+
+def render_the_zone(raw, ax_name):
+    front = lax.axis_index(ax_name)
+    oldest = lax.axis_size(ax_name)
+    step_out, q_next, y2 = (oldest, front, raw.shape[0])
+    y_new, local_out = (raw, 1)
+    while local_out < step_out:
+        y_new = jnp.concatenate(
+            [
+                y_new,
+                lax.ppermute(
+                    y_new,
+                    axis_name=ax_name,
+                    perm=[(ix, (ix - local_out) % step_out) for ix in range(step_out)],
+                ),
+            ],
+            0,
+        )
+        local_out = 2 * local_out
+    y = jnp.roll(y_new, shift=q_next * y2, axis=0)
+    return y
 
 
 def cosine_table(length):
@@ -36,7 +58,7 @@
 def shards(cond_orbitals, cond_energy, val_orbitals, val_energy, val_slots, owner_count):
     cond_block = lax.all_to_all(cond_orbitals, "pair", split_axis=2, concat_axis=1, tiled=True)[0].T
     all_orb, all_energy = (
-        lax.all_gather(val_orbitals, ("ka", "pair"), axis=0, tiled=True),
+        render_the_zone(val_orbitals, ("ka", "pair")),
         lax.all_gather(val_energy, ("ka", "pair"), axis=0, tiled=True),
     )
     slots = val_slots[0, 0]

time: 299 us -> 256 us (0.86)
  blocking collectives: 108 us -> 41.5 us
  waiting for transfers between devices: 92.6 us -> 109 us
  starting transfers between devices: 8.38 us -> 11.5 us
    all_gather x1 -> x0, blocking collectives: 67.5 us -> none  [shards(): lax.all_gather(val_orbitals, ('ka', 'pair'), axis=0, tiled=True)]
    ppermute x0 -> x5, waiting for transfers between devices: none -> 11.8 us  [render_the_zone(): lax.ppermute(y_new, axis_name=ax_name, perm=[(ix, (ix - local_out) % step...]
    ppermute x0 -> x5, starting transfers between devices: none -> 7.9 us  [render_the_zone(): lax.ppermute(y_new, axis_name=ax_name, perm=[(ix, (ix - local_out) % step...]
    reduce_scatter x1, waiting for transfers between devices: 92.6 us -> 97.6 us  [shards(): lax.psum_scatter(lax.dot_general(moved, weighted, (((0,), (0,)), ((), ())...]
    all_to_all x1, starting transfers between devices: 8.34 us -> 3.57 us  [shards(): lax.all_to_all(cond_orbitals, 'pair', split_axis=2, concat_axis=1, tiled=...]
    unnamed x8 -> x7, local copies, waits for them, and re-layouts: 15.4 us -> 15.3 us
  transfers between devices with their start and end apart: 2 -> 7, of which waited for: 1 -> 5; matrix products, arithmetic and copies ran while one was open for 1% -> 9% of each run, Pallas kernels for 0% -> 0%
where the time goes in v1:
time: 256 us; the launch traced here: 255 us
  waiting for transfers between devices  109 us (43%)
  blocking collectives  41.5 us (16%)
  local copies, waits for them, and re-layouts  33.1 us (13%)
  other arithmetic  23 us (9%)
  matrix products  22.1 us (9%)
  between operations  14.9 us (6%)
  starting transfers between devices  11.5 us (4%)
    reduce_scatter x1, waiting for transfers between devices, shards(): lax.psum_scatter(lax.dot_general(moved, weighted, (((0,), (0,)), ((), ())...  97.6 us
    unnamed x1, blocking collectives  41.5 us
    unnamed x7, local copies, waits for them, and re-layouts  15.3 us
    convert_element_type x1, local copies, waits for them, and re-layouts, owner_terms(): pair_real = (picked[:, None, :].astype(jnp.float32) * cond_block[None].as...  13.5 us
    ppermute x5, waiting for transfers between devices, render_the_zone(): lax.ppermute(y_new, axis_name=ax_name, perm=[(ix, (ix - local_out) % step...  11.8 us
    unnamed x1, other arithmetic  11.5 us
    dot_general x1, matrix products, shards(): lax.dot_general(moved, weighted, (((0,), (0,)), ((), ())), preferred_elem...  10.6 us
    ppermute x5, starting transfers between devices, render_the_zone(): lax.ppermute(y_new, axis_name=ax_name, perm=[(ix, (ix - local_out) % step...  7.9 us
  transfers between devices with their start and end apart: 7, of which 5 were waited for; matrix products, arithmetic and copies ran while one was open for 9% of the time, Pallas kernels for 0%

profile of v1, /device:TPU:0, one launch (start us, length us, event | category | flops | bytes accessed | tf_op | source)
XLA Modules:
  0.0 255.4 jit_solution(10145907756838634918)
XLA Ops:
  6.5 6.4 %collective-permute-start = (bf16[1,2048]{1,0:T(2,128)(2,1)}, bf16[1,2048]{1,0:T(2,128)(2,1)S(1)}, u32[]{:S(2)}, u32[]{:S(2)}) collective-permute-start(bf16[1,2048]{1,0:T(2,128)(2,1)} %param.8), channel_id=1, source_target_pairs={{0,31},{1,0},{2,1},{3,2},{4,3},{5,4},{6,5},{7,6},{8,7},{9,8},{10,9... | collective-permute-start | bytes 12296 | tf_op jit(solution)/shard_map/ppermute | solution.py:22
  12.9 2.3 copy.11
  15.3 0.5 broadcast.174
  15.8 11.5 %reduce = bf16[2048,128]{1,0:T(8,128)(2,1)S(1)} reduce(bf16[2048,1,128]{2,1,0:T(2,128)(2,1)S(1)} %bitcast.39, bf16[]{:T(256)} %broadcast.174), dimensions={1}, to_apply=%bitcast.27.reduce_sub_computation | reduce | bytes 1048578
  27.3 0.9 reshape.160
  28.3 3.6 %all-to-all-start = ((bf16[16,2,8192]{2,1,0:T(2,128)(2,1)}), bf16[16,2,8192]{2,1,0:T(2,128)(2,1)S(1)}, u32[]{:S(2)}, u32[]{:S(2)}) async-start(bf16[16,2,8192]{2,1,0:T(2,128)(2,1)} %reshape.160), calls=%async_computation | async-start | bytes 1048576 | tf_op jit(solution)/shard_map/all_to_all | solution.py:59
  31.8 0.0 reduce-scatter.2.cloned.1.call-start
  31.9 0.7 fusion.11
  33.2 0.1 dynamic-update-slice
  33.4 41.5 %all-reduce = bf16[32]{0:T(256)(128)(2,1)S(1)} all-reduce(bf16[32]{0:T(256)(128)(2,1)S(1)} %dynamic-update-slice), channel_id=1, replica_groups=mesh['ka'=2,'pair'=16] {'ka','pair'}, use_global_device_ids=true, to_apply=%add | all-reduce | flops 32 | bytes 128
  74.8 0.7 gather_fusion.1
  75.5 0.7 select_convert_fusion.1
  76.8 0.0 collective-permute-done
  76.8 0.7 pad_maximum_fusion.2
  77.5 1.3 collective-permute-start.1
  78.8 2.7 %collective-permute-done.1 = bf16[2,2048]{1,0:T(2,128)(2,1)S(1)} collective-permute-done((bf16[2,2048]{1,0:T(2,128)(2,1)S(1)}, bf16[2,2048]{1,0:T(2,128)(2,1)S(1)}, u32[]{:S(2)}, u32[]{:S(2)}) %collective-permute-start.1) | collective-permute-done | bytes 8224 | tf_op jit(solution)/shard_map/ppermute | solution.py:22
  81.5 0.7 pad_maximum_fusion.1
  82.2 0.1 collective-permute-start.2
  82.3 0.7 divide_bitcast_fusion
  83.0 3.1 %collective-permute-done.2 = bf16[4,2048]{1,0:T(4,128)(2,1)S(1)} collective-permute-done((bf16[4,2048]{1,0:T(4,128)(2,1)S(1)}, bf16[4,2048]{1,0:T(4,128)(2,1)S(1)}, u32[]{:S(2)}, u32[]{:S(2)}) %collective-permute-start.2) | collective-permute-done | bytes 16416 | tf_op jit(solution)/shard_map/ppermute | solution.py:22
  86.1 0.7 pad_maximum_fusion
  86.9 0.1 collective-permute-start.3
  87.0 4.8 %collective-permute-done.3 = bf16[8,2048]{1,0:T(8,128)(2,1)S(1)} collective-permute-done((bf16[8,2048]{1,0:T(8,128)(2,1)S(1)}, bf16[8,2048]{1,0:T(8,128)(2,1)S(1)}, u32[]{:S(2)}, u32[]{:S(2)}) %collective-permute-start.3) | collective-permute-done | bytes 32800 | tf_op jit(solution)/shard_map/ppermute | solution.py:22
  91.7 0.7 concatenate.25
  92.5 0.1 collective-permute-start.4
  92.6 1.2 collective-permute-done.4
  93.8 1.5 concatenate.26
  95.4 0.6 gather_fusion
  96.0 0.1 select_convert_fusion
  96.1 0.0 all-to-all-done
  96.1 0.5 reshape.161
  96.6 0.1 copy.12
  96.7 0.1 convert_bitcast_fusion
  96.8 0.3 copy.13
  97.1 0.3 copy.14
  97.5 5.4 %multiply_convert_fusion = bf16[16,128,2048]{2,1,0:T(8,128)(2,1)} fusion(f32[128,2048]{1,0:T(8,128)S(1)} %copy.14, f32[16,2048]{1,0:T(8,128)S(1)} %select_convert_fusion), kind=kLoop, calls=%fused_computation.3 | loop fusion | flops 8388608 | bytes 9568256 | tf_op jit(solution)/shard_map/convert_element_type | solution.py:46
  102.8 13.5 %convert_element_type.68 = bf16[32768,128]{1,0:T(8,128)(2,1)} reshape(bf16[16,128,2048]{2,1,0:T(8,128)(2,1)} %multiply_convert_fusion) | data formatting | bytes 16777216 | tf_op jit(solution)/shard_map/convert_element_type | solution.py:46
  116.3 5.9 %convolution_convert_fusion = bf16[32768,128]{1,0:T(8,128)(2,1)S(1)} fusion(bf16[32768,128]{1,0:T(8,128)(2,1)} %convert_element_type.68, f32[128]{0:T(128)S(1)} %get-tuple-element.8, f32[128]{0:T(128)S(1)} %get-tuple-element.7), kind=kOutput, calls=%fused_computation.2 | convolution fusion | flops 1078001664 | bytes 16778240 | tf_op jit(solution)/shard_map/dot_general | solution.py:49
  122.2 5.6 %convolution_convert_fusion.1 = bf16[2048,128,16]{1,2,0:T(8,128)(2,1)} fusion(bf16[2048,16,128]{2,1,0:T(8,128)(2,1)S(1)} %bitcast.35, f32[16]{0:T(128)S(1)} %get-tuple-element.10, f32[16]{0:T(128)S(1)} %get-tuple-element.9), kind=kOutput, calls=%fused_computation.5 | convolution fusion | flops 138413056 | bytes 16777344 | tf_op jit(solution)/shard_map/ja,pak->pjk/dot_general | solution.py:51
  127.8 10.9 %copy.17 = bf16[256,8,16,128]{3,1,2,0:T(8,128)(2,1)} copy(bf16[256,8,16,128]{3,2,1,0:T(8,128)(2,1)} %bitcast.36) | data formatting | bytes 16777216
  138.7 10.6 %fusion = f32[2048,512]{1,0:T(8,128)} fusion(bf16[2048,2048]{1,0:T(8,128)(2,1)} %bitcast.37, f32[2048]{0:T(1024)S(1)} %divide_bitcast_fusion), kind=kOutput, calls=%fused_computation.7 | convolution fusion | flops 4298113024 | bytes 14688256 | tf_op jit(solution)/shard_map/dot_general | solution.py:73
  149.3 0.0 reduce-scatter.2.cloned.1.call-update
  149.3 97.6 %reduce-scatter.2.cloned.1.call-done = f32[128,512]{1,0:T(8,128)} async-done(((f32[2048,512]{1,0:T(8,128)}), f32[128,512]{1,0:T(8,128)}) %reduce-scatter.2.cloned.1.call-update) | async-done | bytes 262160 | tf_op jit(solution)/shard_map/reduce_scatter | solution.py:72
  246.9 1.7 multiply_bitcast_fusion
  (6 shorter events, 0.1 us)
Async XLA Ops:
  6.5 70.3 %collective-permute-start = (bf16[1,2048]{1,0:T(2,128)(2,1)}, bf16[1,2048]{1,0:T(2,128)(2,1)S(1)}, u32[]{:S(2)}, u32[]{:S(2)}) collective-permute-start(bf16[1,2048]{1,0:T(2,128)(2,1)} %param.8), channel_id=1, source_target_pairs={{0,31},{1,0},{2,1},{3,2},{4,3},{5,4},{6,5},{7,6},{8,7},{9,8},{10,9... | collective-permute-start | bytes 12296 | tf_op jit(solution)/shard_map/ppermute | solution.py:22
  28.3 67.8 %all-to-all-start = ((bf16[16,2,8192]{2,1,0:T(2,128)(2,1)}), bf16[16,2,8192]{2,1,0:T(2,128)(2,1)S(1)}, u32[]{:S(2)}, u32[]{:S(2)}) async-start(bf16[16,2,8192]{2,1,0:T(2,128)(2,1)} %reshape.160), calls=%async_computation | async-start | bytes 1048576 | tf_op jit(solution)/shard_map/all_to_all | solution.py:59
  31.8 215.0 %reduce-scatter.2.cloned.1.call-start = ((), (), s32[]{:S(2)}) async-start(), calls=%async_computation.2 | async-start | bytes 4456448 | tf_op jit(solution)/shard_map/reduce_scatter | solution.py:72
  77.5 4.0 %collective-permute-start.1 = (bf16[2,2048]{1,0:T(2,128)(2,1)S(1)}, bf16[2,2048]{1,0:T(2,128)(2,1)S(1)}, u32[]{:S(2)}, u32[]{:S(2)}) collective-permute-start(bf16[2,2048]{1,0:T(2,128)(2,1)S(1)} %pad_maximum_fusion.2), channel_id=1, source_target_pairs={{0,30},{1,31},{2,0},{3,1},{4,2},{5,3},{6,4},{7,5},{8,6},{9,7},{10,... | collective-permute-start | bytes 24584 | tf_op jit(solution)/shard_map/ppermute | solution.py:22
  82.2 3.9 %collective-permute-start.2 = (bf16[4,2048]{1,0:T(4,128)(2,1)S(1)}, bf16[4,2048]{1,0:T(4,128)(2,1)S(1)}, u32[]{:S(2)}, u32[]{:S(2)}) collective-permute-start(bf16[4,2048]{1,0:T(4,128)(2,1)S(1)} %pad_maximum_fusion.1), channel_id=1, source_target_pairs={{0,28},{1,29},{2,30},{3,31},{4,0},{5,1},{6,2},{7,3},{8,4},{9,5},{1... | collective-permute-start | bytes 49160 | tf_op jit(solution)/shard_map/ppermute | solution.py:22
  86.9 4.9 %collective-permute-start.3 = (bf16[8,2048]{1,0:T(8,128)(2,1)S(1)}, bf16[8,2048]{1,0:T(8,128)(2,1)S(1)}, u32[]{:S(2)}, u32[]{:S(2)}) collective-permute-start(bf16[8,2048]{1,0:T(8,128)(2,1)S(1)} %pad_maximum_fusion), channel_id=1, source_target_pairs={{0,24},{1,25},{2,26},{3,27},{4,28},{5,29},{6,30},{7,31},{8,0},{9,1... | collective-permute-start | bytes 98312 | tf_op jit(solution)/shard_map/ppermute | solution.py:22
  92.5 1.3 collective-permute-start.4
Sparse Core Ops, SparseCore 0:
  149.4 97.3 reduce-scatter.1
